TPU v7x, 128 devices: a whole 4x4x4 slice. The times are simulated.
128 devices in a mesh: blk: 32 (over x, y_hi, z), grp: 4 (over y_lo, core).
Axes of the slice: x: 4, y: 4 (y_hi: 2, y_lo: 2; y = y_hi * 2 + y_lo), z: 4, core: 2. Of those that a mesh axis runs over, the one named last changes fastest.
Arguments:
- amplitudes: bfloat16 [1920, 1920], P('blk'), may hold values from -6 to 6
- hole_panel: bfloat16 [1920, 32, 1920], P(None, 'blk', 'grp'), may hold values from -0.375 to 0.375
- virt_fock: bfloat16 [1920, 1920], replicated, may hold values from -0.125 to 0.125
- irrep_sizes: int32 [8], replicated, may hold values from 1 to 480, 1920 in all
- pair_irreps: int32 [32], P('blk'), may hold values from 0 to 7
Outputs:
- dressed: bfloat16 [1920, 32, 1920], P('grp', 'blk')
Inputs may be any that keep to these rules, and one draw needn't show every extreme that they name: `irrep_sizes`: the 8 entries sum to 1920.
All inputs are finite; a program needn't handle non-finite values.
Results may differ from a plain program's by a relative error of at most 0.0049.
Values may be sent and summed in bfloat16 or wider, within the bound.
A program may use at most 128 MiB of HBM per device.

v0:
```python
import jax
import jax.numpy as jnp
from jax import lax
from jax.sharding import PartitionSpec as P


def irrep_of(positions, block_sizes):
    bounds = jnp.cumsum(block_sizes)[:-1]
    return jnp.sum((positions[:, None] >= bounds[None, :]).astype(jnp.int32), axis=1)


def local(amplitudes, hole_panel, virt_fock, irrep_sizes, pair_irreps):
    virtuals = amplitudes.shape[1]
    occ_local = hole_panel.shape[1]
    quarter = hole_panel.shape[2]
    col_start = lax.axis_index("grp") * quarter
    rows_irrep = irrep_of(jnp.arange(virtuals, dtype=jnp.int32), irrep_sizes)
    cols_irrep = irrep_of(col_start + jnp.arange(quarter, dtype=jnp.int32), irrep_sizes)
    allowed = (
        jnp.bitwise_xor(rows_irrep[:, None, None], cols_irrep[None, None, :])
        == pair_irreps[None, :, None]
    )
    masked = jnp.where(allowed, hole_panel, jnp.zeros((), jnp.bfloat16))
    flattened = masked.reshape(virtuals, occ_local * quarter)
    coupled = jnp.dot(
        lax.all_gather(amplitudes, "blk", axis=0, tiled=True),
        flattened,
        preferred_element_type=jnp.float32,
    ).astype(jnp.bfloat16)
    coupled = coupled.reshape(virtuals, occ_local, quarter)
    fock_rows = lax.dynamic_slice_in_dim(virt_fock, col_start, quarter, 0)
    summed = lax.psum_scatter(
        jnp.einsum("ajb,be->aje", coupled, fock_rows, preferred_element_type=jnp.float32),
        "grp",
        scatter_dimension=0,
        tiled=True,
    )
    return summed.astype(jnp.bfloat16)


def solution(mesh):
    in_specs = (P("blk", None), P(None, "blk", "grp"), P(), P(), P("blk"))
    out_specs = P("grp", "blk", None)
    return jax.shard_map(local, mesh=mesh, in_specs=in_specs, out_specs=out_specs, check_vma=False)
```

profile of v0, /device:TPU:1, one launch (start us, length us, event | category | flops | bytes accessed | tf_op | source)
XLA Modules:
  0.0 277.2 jit_solution(7345954068258640997)
XLA Ops:
  6.5 0.0 all-gather.3.cloned.1.call-start
  6.5 0.7 all-gather.3.cloned.1.call-update
  7.3 0.0 reduce-scatter.2.cloned.1.call-start
  8.0 0.8 reduce-window.4
  8.8 0.1 convert_reduce_fusion
  8.9 0.1 convert_reduce_fusion.1
  9.0 0.0 copy-start
  9.0 105.4 %all-gather.3.cloned.1.call-done = bf16[32,60,1920]{2,1,0:T(8,128)(2,1)} async-done(((bf16[1,60,1920]{2,1,0:T(8,128)(2,1)}), bf16[32,60,1920]{2,1,0:T(8,128)(2,1)}) %all-gather.3.cloned.1.call-update) | async-done | bytes 7372816 | tf_op jit(solution)/shard_map/all_gather | solution.py:26
  114.4 8.9 %reshape.72 = bf16[1920,1920]{1,0:T(8,128)(2,1)} reshape(bf16[32,60,1920]{2,1,0:T(8,128)(2,1)} %all-gather.3.cloned.1.call-done) | data formatting | bytes 14745600
  123.3 0.0 copy-done
  123.3 14.5 %convolution_bitcast_fusion = f32[1920,1,1920]{2,0,1:T(8,128)} fusion(bf16[1920,1920]{1,0:T(8,128)(2,1)} %param.7, s32[]{:T(128)S(6)} %select_n.8, bf16[1920,1920]{1,0:T(8,128)(2,1)} %reshape.72, bf16[1920,1,480]{0,2,1:T(8,128)(2,1)S(1)} %copy-done, s32[]{:T(128)} %bitcast.13, s32[480]{0:T(512)S(1)} %convert_reduce_fusion.1, s32[1920]{0:T(1024)S(1)} %convert_reduce_fusion), kind=kOutput, calls=%fused_computation | convolution fusion | flops 7081574400 | bytes 25814916 | tf_op jit(solution)/shard_map/ajb,be->aje/dot_general | solution.py:33
  137.8 0.0 reduce-scatter.2.cloned.1.call-update
  137.8 129.1 %reduce-scatter.2.cloned.1.call-done = f32[480,1,1920]{2,0,1:T(8,128)} async-done(((f32[1920,1,1920]{2,0,1:T(8,128)}), f32[480,1,1920]{2,0,1:T(8,128)}) %reduce-scatter.2.cloned.1.call-update) | async-done | bytes 3686416 | tf_op jit(solution)/shard_map/reduce_scatter | solution.py:32
  266.9 3.5 %convert_element_type.16 = bf16[480,1,1920]{2,0,1:T(8,128)(2,1)} convert(f32[480,1,1920]{2,0,1:T(8,128)} %reduce-scatter.2.cloned.1.call-done) | non-fusion elementwise | flops 921600 | bytes 5529600 | tf_op jit(solution)/shard_map/convert_element_type | solution.py:38
  (2 shorter events, 0.0 us)
Async XLA Ops:
  6.5 107.9 %all-gather.3.cloned.1.call-start = ((), (), s32[]{:S(2)}) async-start(), calls=%async_computation.2 | async-start | bytes 8110080 | tf_op jit(solution)/shard_map/all_gather | solution.py:26
  7.3 259.7 %reduce-scatter.2.cloned.1.call-start = ((), (), s32[]{:S(2)}) async-start(), calls=%async_computation.1 | async-start | bytes 18432000 | tf_op jit(solution)/shard_map/reduce_scatter | solution.py:32
  9.0 114.3 %copy-start = (bf16[1920,1,480]{0,2,1:T(8,128)(2,1)S(1)}, bf16[1920,1,480]{0,2,1:T(8,128)(2,1)}, u32[]{:S(2)}) copy-start(bf16[1920,1,480]{0,2,1:T(8,128)(2,1)} %param.6) | copy-start | bytes 5529604
Sparse Core Ops, SparseCore 0:
  10.3 104.0 all-gather.2
  137.9 128.9 reduce-scatter.1
where the time goes:
time: 278 us; the launch traced here: 277 us
  waiting for transfers between devices  235 us (85%)
  matrix products  14.5 us (5%)
  between operations  14.1 us (5%)
  local copies, waits for them, and re-layouts  8.89 us (3%)
  other arithmetic  4.48 us (2%)
    reduce_scatter x1, waiting for transfers between devices, local(): lax.psum_scatter(jnp.einsum('ajb,be->aje', coupled, fock_rows, preferred_...  129 us
    all_gather x1, waiting for transfers between devices, local(): lax.all_gather(amplitudes, 'blk', axis=0, tiled=True)  105 us
    dot_general x1, matrix products, local(): jnp.einsum('ajb,be->aje', coupled, fock_rows, preferred_element_type=jnp....  14.5 us
    unnamed x3, local copies, waits for them, and re-layouts  8.89 us
  transfers between devices with their start and end apart: 2, of which 2 were waited for; matrix products, arithmetic and copies ran while one was open for 0% of the time, Pallas kernels for 0%

commit v1 on v0

--- a/solution.py
+++ b/solution.py
@@ -23,7 +23,9 @@
     masked = jnp.where(allowed, hole_panel, jnp.zeros((), jnp.bfloat16))
     flattened = masked.reshape(virtuals, occ_local * quarter)
     coupled = jnp.dot(
-        lax.all_gather(amplitudes, "blk", axis=0, tiled=True),
+        jnp.concatenate(
+            lax.all_to_all(jnp.stack([amplitudes] * lax.axis_size("blk")), "blk", 0, 0), axis=0
+        ),
         flattened,
         preferred_element_type=jnp.float32,
     ).astype(jnp.bfloat16)

time: 278 us -> 309 us (1.11)
  waiting for transfers between devices: 235 us -> 250 us
  starting transfers between devices: 0.04 us -> 11.6 us
  local copies, waits for them, and re-layouts: 8.89 us -> 14.1 us
    all_to_all x0 -> x1, waiting for transfers between devices: none -> 115 us  [local(): lax.all_to_all(jnp.stack([amplitudes] * lax.axis_size('blk')), 'blk', 0, 0)]
    all_gather x1 -> x0, waiting for transfers between devices: 105 us -> none  [local(): lax.all_gather(amplitudes, 'blk', axis=0, tiled=True)]
    all_to_all x0 -> x1, starting transfers between devices: none -> 11.6 us  [local(): lax.all_to_all(jnp.stack([amplitudes] * lax.axis_size('blk')), 'blk', 0, 0)]
    reshape x0 -> x1, local copies, waits for them, and re-layouts: none -> 8.88 us  [local(): jnp.concatenate(lax.all_to_all(jnp.stack([amplitudes] * lax.axis_size('bl...]
    unnamed x3 -> x4, local copies, waits for them, and re-layouts: 8.89 us -> 0.01 us
    reduce_scatter x1, waiting for transfers between devices: 129 us -> 136 us  [local(): lax.psum_scatter(jnp.einsum('ajb,be->aje', coupled, fock_rows, preferred_...]
    another operation x0 -> x1, local copies, waits for them, and re-layouts: none -> 5.17 us  [local(): jnp.stack([amplitudes] * lax.axis_size('blk'))]
where the time goes in v1:
time: 309 us; the launch traced here: 308 us
  waiting for transfers between devices  250 us (81%)
  matrix products  14.5 us (5%)
  local copies, waits for them, and re-layouts  14.1 us (5%)
  between operations  14.1 us (5%)
  starting transfers between devices  11.6 us (4%)
  other arithmetic  3.83 us (1%)
    reduce_scatter x1, waiting for transfers between devices, local(): lax.psum_scatter(jnp.einsum('ajb,be->aje', coupled, fock_rows, preferred_...  136 us
    all_to_all x1, waiting for transfers between devices, local(): lax.all_to_all(jnp.stack([amplitudes] * lax.axis_size('blk')), 'blk', 0, 0)  115 us
    dot_general x1, matrix products, local(): jnp.einsum('ajb,be->aje', coupled, fock_rows, preferred_element_type=jnp....  14.5 us
    all_to_all x1, starting transfers between devices, local(): lax.all_to_all(jnp.stack([amplitudes] * lax.axis_size('blk')), 'blk', 0, 0)  11.6 us
    reshape x1, local copies, waits for them, and re-layouts, local(): jnp.concatenate(lax.all_to_all(jnp.stack([amplitudes] * lax.axis_size('bl...  8.88 us
  transfers between devices with their start and end apart: 2, of which 2 were waited for; matrix products, arithmetic and copies ran while one was open for 0% of the time, Pallas kernels for 0%

profile of v1, /device:TPU:1, one launch (start us, length us, event | category | flops | bytes accessed | tf_op | source)
XLA Modules:
  0.0 308.5 jit_solution(11501701752757648630)
XLA Ops:
  6.5 5.2 %stack.2 = bf16[32,60,1920]{2,1,0:T(8,128)(2,1)} broadcast(bf16[60,1920]{1,0:T(8,128)(2,1)} %param.5), dimensions={1,2} | broadcast | bytes 7603200 | tf_op jit(solution)/shard_map/stack | solution.py:27
  11.7 0.0 copy-start.1
  11.7 11.6 %all-to-all-start = ((bf16[32,60,1920]{2,1,0:T(8,128)(2,1)}), bf16[32,60,1920]{2,1,0:T(8,128)(2,1)}, u32[]{:S(2)}, u32[]{:S(2)}) async-start(bf16[32,60,1920]{2,1,0:T(8,128)(2,1)} %stack.2), calls=%async_computation | async-start | bytes 15728640 | tf_op jit(solution)/shard_map/all_to_all | solution.py:27
  23.3 0.0 reduce-scatter.2.cloned.1.call-start
  24.0 0.0 copy-done.1
  24.0 0.2 reduce-window.4
  24.2 0.1 convert_reduce_fusion
  24.3 0.1 convert_reduce_fusion.1
  24.4 0.0 copy-start
  24.4 114.7 %all-to-all-done = bf16[32,60,1920]{2,1,0:T(8,128)(2,1)} async-done(((bf16[32,60,1920]{2,1,0:T(8,128)(2,1)}), bf16[32,60,1920]{2,1,0:T(8,128)(2,1)}, u32[]{:S(2)}, u32[]{:S(2)}) %all-to-all-start) | async-done | bytes 7372832 | tf_op jit(solution)/shard_map/all_to_all | solution.py:27
  139.1 8.9 %reshape.76 = bf16[1920,1920]{1,0:T(8,128)(2,1)} reshape(bf16[32,60,1920]{2,1,0:T(8,128)(2,1)} %all-to-all-done) | data formatting | bytes 14745600 | tf_op jit(solution)/shard_map/reshape | solution.py:26
  148.0 0.0 copy-done
  148.0 14.5 %convolution_bitcast_fusion = f32[1920,1,1920]{2,0,1:T(8,128)} fusion(bf16[1920,1920]{1,0:T(8,128)(2,1)} %param.7, s32[]{:T(128)S(6)} %select_n.8, bf16[1920,1920]{1,0:T(8,128)(2,1)} %reshape.76, bf16[1920,1,480]{0,2,1:T(8,128)(2,1)S(1)} %copy-done, s32[]{:T(128)} %bitcast.12, s32[480]{0:T(512)S(1)} %convert_reduce_fusion.1, s32[1920]{0:T(1024)S(1)} %convert_reduce_fusion), kind=kOutput, calls=%fused_computation | convolution fusion | flops 7081574400 | bytes 25814916 | tf_op jit(solution)/shard_map/ajb,be->aje/dot_general | solution.py:35
  162.5 0.0 reduce-scatter.2.cloned.1.call-update
  162.5 135.7 %reduce-scatter.2.cloned.1.call-done = f32[480,1,1920]{2,0,1:T(8,128)} async-done(((f32[1920,1,1920]{2,0,1:T(8,128)}), f32[480,1,1920]{2,0,1:T(8,128)}) %reduce-scatter.2.cloned.1.call-update) | async-done | bytes 3686416 | tf_op jit(solution)/shard_map/reduce_scatter | solution.py:34
  298.2 3.5 %convert_element_type.16 = bf16[480,1,1920]{2,0,1:T(8,128)(2,1)} convert(f32[480,1,1920]{2,0,1:T(8,128)} %reduce-scatter.2.cloned.1.call-done) | non-fusion elementwise | flops 921600 | bytes 5529600 | tf_op jit(solution)/shard_map/convert_element_type | solution.py:40
  (2 shorter events, 0.0 us)
Async XLA Ops:
  11.7 12.3 %copy-start.1 = (s32[8]{0:T(128)S(1)}, s32[8]{0:T(128)}, u32[]{:S(2)}) copy-start(s32[8]{0:T(128)} %param.8) | copy-start | bytes 100
  11.7 127.4 %all-to-all-start = ((bf16[32,60,1920]{2,1,0:T(8,128)(2,1)}), bf16[32,60,1920]{2,1,0:T(8,128)(2,1)}, u32[]{:S(2)}, u32[]{:S(2)}) async-start(bf16[32,60,1920]{2,1,0:T(8,128)(2,1)} %stack.2), calls=%async_computation | async-start | bytes 15728640 | tf_op jit(solution)/shard_map/all_to_all | solution.py:27
  23.3 274.9 %reduce-scatter.2.cloned.1.call-start = ((), (), s32[]{:S(2)}) async-start(), calls=%async_computation.2 | async-start | bytes 18432000 | tf_op jit(solution)/shard_map/reduce_scatter | solution.py:34
  24.4 123.6 %copy-start = (bf16[1920,1,480]{0,2,1:T(8,128)(2,1)S(1)}, bf16[1920,1,480]{0,2,1:T(8,128)(2,1)}, u32[]{:S(2)}) copy-start(bf16[1920,1,480]{0,2,1:T(8,128)(2,1)} %param.6) | copy-start | bytes 5529604
Sparse Core Ops, SparseCore 0:
  162.6 135.5 reduce-scatter.1
